TPU v7x, 32 devices: a whole 2x2x4 slice. The times are simulated.
32 devices in a mesh: parts: 2 (over y), row: 4 (over z), col: 4 (over x, core).
Axes of the slice: x: 2, y: 2, z: 4, core: 2. Of those that a mesh axis runs over, the one named last changes fastest.
Arguments:
- amplitudes: bfloat16 [8, 100, 512, 512], P('parts', 'col', 'row'), parts along dimension 0, may hold values from -12 to 12
- integrals: bfloat16 [200, 512, 512], P(('parts', 'col'), 'row'), parts along dimension 0, may hold values from -0.109375 to 0.109375
- occ_irrep: int32 [200], P('parts'), parts along dimension 0, may hold values from 0 to 7, as said below
- vir_irrep: int32 [1024], P('parts'), parts along dimension 0, may hold values from 0 to 7, as said below
- screen: int32 [200, 8], P('parts'), parts along dimension 0, may hold values 0 or 1
- occ_energy: float32 [200], P('parts'), parts along dimension 0, may hold values from -1 to -0.3
- vir_energy: float32 [1024], P('parts'), parts along dimension 0, may hold values from 0.1 to 1
Outputs:
- update: float32 [512, 8, 512], P('row', 'parts', 'col'), parts along dimension 1
There are 2 independent parts, one for each index of `parts`. A program takes and returns all parts, laid end to end along the dimension named above; each array names one. Nothing has to cross between parts.
Inputs may be any that keep to these rules, and one draw needn't show every extreme that they name: `occ_irrep`: the labels never fall from one orbital to the next; the first is 0 and the last is 7. `vir_irrep`: the labels never fall from one orbital to the next and every label from 0 to 7 occurs; exactly one label covers 256 virtual orbitals, every other label fewer.
All inputs are finite; a program needn't handle non-finite values.
Results may differ from a plain program's by a relative error of at most 0.0003.
Values may be sent and summed in bfloat16 or wider, within the bound.
A program may use at most 128 MiB of HBM per device.

v0:
```python
import jax
import jax.numpy as jnp
from jax import lax
from jax.sharding import PartitionSpec as P


def parity(first_label, second_label, third_label, fourth_label):
    return jnp.bitwise_xor(
        jnp.bitwise_xor(first_label, second_label), jnp.bitwise_xor(third_label, fourth_label)
    )


def on_device(amplitudes, integrals, occ_irrep, vir_irrep, screen, occ_energy, vir_energy):
    row_count = lax.axis_size("row")
    column_count = lax.axis_size("col")
    batch_size, occ_share, vir_share, vir_total = amplitudes.shape
    occ_total = occ_irrep.shape[0]
    occ_offset = lax.axis_index("col") * occ_share
    vir_offset = lax.axis_index("row") * vir_share
    occ_local = lax.dynamic_slice_in_dim(occ_irrep, occ_offset, occ_share)
    vir_local = lax.dynamic_slice_in_dim(vir_irrep, vir_offset, vir_share)
    pair_label = occ_irrep[batch_size]
    keep_amp = (
        parity(
            occ_irrep[:batch_size, None, None, None],
            occ_local[None, :, None, None],
            vir_local[None, None, :, None],
            vir_irrep[None, None, None, :],
        )
        == 0
    )
    amp_kept = jnp.where(keep_amp, amplitudes, jnp.zeros_like(amplitudes))
    irrep_codes = jnp.arange(8, dtype=jnp.int32)
    screen_rows = lax.dynamic_slice_in_dim(screen, occ_offset, occ_share, 0)
    screen_local = jnp.sum(
        screen_rows[:, None, :] * (vir_local[None, :, None] == irrep_codes).astype(jnp.int32),
        axis=2,
    )
    keep_int = (
        parity(
            occ_local[:, None, None], vir_local[None, :, None], pair_label, vir_irrep[None, None, :]
        )
        == 0
    ) & (screen_local[:, :, None] == 1)
    int_kept = jnp.where(keep_int, integrals, jnp.zeros_like(integrals))
    packed = amp_kept.reshape(batch_size, occ_share, vir_share, row_count, vir_share)
    packed = jnp.transpose(packed, (3, 1, 0, 4, 2)).reshape(
        row_count, occ_share, batch_size * vir_share * vir_share
    )
    arrived = lax.all_to_all(
        lax.all_to_all(packed, "row", split_axis=0, concat_axis=0, tiled=True),
        "col",
        split_axis=0,
        concat_axis=1,
        tiled=True,
    )
    block_count = row_count // column_count
    vir_columns = block_count * vir_share
    arranged = arrived.reshape(block_count, occ_total, batch_size, vir_share, vir_share)
    arranged = jnp.transpose(arranged, (1, 3, 2, 0, 4)).reshape(
        occ_total, vir_share, batch_size, vir_columns
    )
    cycle_whole = lax.dot_general(
        lax.all_gather(int_kept, "col", axis=0, tiled=True),
        arranged,
        (((0, 1), (0, 1)), ((), ())),
        preferred_element_type=jnp.float32,
    )
    cycle_mine = lax.psum_scatter(cycle_whole, "row", scatter_dimension=0, tiled=True)
    energy_cols = lax.dynamic_slice_in_dim(
        vir_energy, lax.axis_index("col") * vir_columns, vir_columns
    )
    energy_rows = lax.dynamic_slice_in_dim(vir_energy, vir_offset, vir_share)
    denominator = (
        occ_energy[:batch_size][None, :, None]
        + occ_energy[batch_size]
        - energy_cols[None, None, :]
        - energy_rows[:, None, None]
    )
    return cycle_mine / denominator


def solution(mesh):
    in_specs = (
        P("parts", "col", "row", None),
        P(("parts", "col"), "row", None),
        P("parts"),
        P("parts"),
        P("parts", None),
        P("parts"),
        P("parts"),
    )
    out_specs = P("row", "parts", "col")
    return jax.shard_map(
        on_device, mesh=mesh, in_specs=in_specs, out_specs=out_specs, check_vma=False
    )
```

profile of v0, /device:TPU:24, one launch (start us, length us, event | category | flops | bytes accessed | tf_op | source)
XLA Modules:
  0.0 716.9 jit_solution(14361143390792385288)
XLA Ops:
  6.5 0.0 copy-start
  6.5 0.8 dynamic_slice.16
  7.3 0.8 broadcast_xor_fusion
  8.1 0.7 dynamic_slice.15
  8.8 0.7 broadcast_xor_fusion.2
  9.5 11.0 %fusion = bf16[4,25,128,512]{3,2,1,0:T(8,128)(2,1)} fusion(bf16[4,25,128,512]{3,2,1,0:T(8,128)(2,1)} %param.7, s32[128,512]{1,0:T(8,128)S(1)} %broadcast_xor_fusion, s32[4,25]{1,0:T(4,128)S(1)} %broadcast_xor_fusion.2), kind=kLoop, calls=%fused_computation.1 | loop fusion | flops 19660800 | bytes 26476944 | tf_op jit(solution)/shard_map/jit(_where)/select_n | solution.py:32
  20.5 18.9 %reshape.174 = bf16[4,25,128,4,128]{4,3,2,1,0:T(4,128)(2,1)} reshape(bf16[4,25,128,512]{3,2,1,0:T(8,128)(2,1)} %fusion) | data formatting | bytes 26214400 | tf_op jit(solution)/shard_map/reshape | solution.py:46
  39.4 20.8 %copy.24 = bf16[4,25,128,4,128]{2,4,0,3,1:T(8,128)(2,1)} copy(bf16[4,25,128,4,128]{4,3,2,1,0:T(4,128)(2,1)} %reshape.174) | data formatting | bytes 26214400 | tf_op jit(solution)/shard_map/reshape | solution.py:46
  60.3 19.7 %reshape.175 = bf16[4,25,65536]{2,0,1:T(4,128)(2,1)} reshape(bf16[4,25,4,128,128]{4,3,2,0,1:T(8,128)(2,1)} %bitcast.25) | data formatting | bytes 26214400 | tf_op jit(solution)/shard_map/reshape | solution.py:47
  80.0 12.7 %copy.25 = bf16[4,25,65536]{2,1,0:T(8,128)(2,1)} copy(bf16[4,25,65536]{2,0,1:T(4,128)(2,1)} %reshape.175) | data formatting | bytes 26214400 | tf_op jit(solution)/shard_map/reshape | solution.py:47
  92.7 0.0 copy-start.5
  92.7 0.0 copy-start.3
  92.7 0.0 copy-start.2
  92.7 7.2 %all-to-all-start = ((bf16[4,25,65536]{2,1,0:T(8,128)(2,1)}), bf16[4,25,65536]{2,1,0:T(8,128)(2,1)}, u32[]{:S(2)}, u32[]{:S(2)}) async-start(bf16[4,25,65536]{2,1,0:T(8,128)(2,1)} %copy.25), calls=%async_computation | async-start | bytes 33554432 | tf_op jit(solution)/shard_map/all_to_all | solution.py:51
  99.9 0.0 all-gather.2.cloned.1.call-start
  100.0 0.0 copy-done.5
  100.0 0.6 slice.12
  100.6 0.0 copy-done
  100.6 0.1 constant_dynamic-slice_fusion
  100.7 0.1 copy.23
  100.8 0.1 multiply_reduce_fusion
  100.9 0.0 copy-done.3
  100.9 0.7 broadcast_xor_fusion.3
  101.5 0.1 broadcast_xor_fusion.1
  101.6 0.0 copy-done.2
  101.6 3.4 fusion.6
  105.0 0.0 all-gather.2.cloned.1.call-update
  105.0 0.0 reduce-scatter.2.cloned.1.call-start
  105.1 355.7 %all-to-all-done = bf16[4,25,65536]{2,1,0:T(8,128)(2,1)} async-done(((bf16[4,25,65536]{2,1,0:T(8,128)(2,1)}), bf16[4,25,65536]{2,1,0:T(8,128)(2,1)}, u32[]{:S(2)}, u32[]{:S(2)}) %all-to-all-start) | async-done | bytes 13107232 | tf_op jit(solution)/shard_map/all_to_all | solution.py:51
  460.8 194.1 %all_to_all.14 = bf16[4,25,65536]{2,1,0:T(8,128)(2,1)} all-to-all(bf16[4,25,65536]{2,1,0:T(8,128)(2,1)} %all-to-all-done), channel_id=1, replica_groups=mesh['parts'=2,'row'=4,'col'=4] {'col'}, dimensions={0} | all-to-all | bytes 26214400 | tf_op jit(solution)/shard_map/all_to_all | solution.py:50
  654.9 13.4 %reshape.176 = bf16[1,100,4,128,128]{4,3,2,1,0:T(8,128)(2,1)} reshape(bf16[4,25,65536]{2,1,0:T(8,128)(2,1)} %all_to_all.14) | data formatting | bytes 26214400 | tf_op jit(solution)/shard_map/reshape | solution.py:59
  668.3 0.0 copy-start.6
  668.3 0.0 copy-start.4
  668.3 0.0 all-gather.2.cloned.1.call-done
  668.3 0.0 copy-start.1
  668.3 14.6 %fusion.7 = f32[512,4,128]{2,0,1:T(8,128)} fusion(bf16[1,100,4,128,128]{4,3,2,1,0:T(8,128)(2,1)} %reshape.176, bf16[100,128,512]{2,1,0:T(8,128)(2,1)} %all-gather.2.cloned.1.call-done), kind=kOutput, calls=%fused_computation.9 | convolution fusion | flops 6710886400 | bytes 27262976 | tf_op jit(solution)/shard_map/dot_general | solution.py:63
  682.9 0.0 reduce-scatter.2.cloned.1.call-update
  682.9 0.0 copy-done.6
  682.9 0.6 slice.15
  683.5 0.0 copy-done.4
  683.5 0.1 fusion.13
  683.6 0.6 slice_add_fusion
  684.3 0.1 broadcast_subtract_fusion
  684.3 23.8 %reduce-scatter.2.cloned.1.call-done = f32[128,4,128]{2,0,1:T(8,128)} async-done(((f32[512,4,128]{2,0,1:T(8,128)}), f32[128,4,128]{2,0,1:T(8,128)}) %reduce-scatter.2.cloned.1.call-update) | async-done | bytes 262160 | tf_op jit(solution)/shard_map/reduce_scatter | solution.py:69
  708.1 1.1 subtract_divide_fusion
  709.2 0.9 copy.28
  710.0 0.0 copy-done.1
  (2 shorter events, 0.0 us)
Async XLA Ops:
  6.5 94.1 %copy-start = (s32[100,8]{0,1:T(8,128)S(1)}, s32[100,8]{0,1:T(8,128)}, u32[]{:S(2)}) copy-start(s32[100,8]{0,1:T(8,128)} %param.11) | copy-start | bytes 9604
  92.7 7.3 %copy-start.5 = (s32[100]{0:T(128)S(1)}, s32[100]{0:T(128)}, u32[]{:S(2)}) copy-start(s32[100]{0:T(128)} %param.9) | copy-start | bytes 1204
  92.7 8.2 %copy-start.3 = (s32[512]{0:T(512)S(1)}, s32[512]{0:T(512)}, u32[]{:S(2)}) copy-start(s32[512]{0:T(512)} %param.10) | copy-start | bytes 6148
  92.7 8.9 %copy-start.2 = (bf16[25,128,512]{2,1,0:T(8,128)(2,1)S(1)}, bf16[25,128,512]{2,1,0:T(8,128)(2,1)}, u32[]{:S(2)}) copy-start(bf16[25,128,512]{2,1,0:T(8,128)(2,1)} %param.8) | copy-start | bytes 9830404
  92.7 368.1 %all-to-all-start = ((bf16[4,25,65536]{2,1,0:T(8,128)(2,1)}), bf16[4,25,65536]{2,1,0:T(8,128)(2,1)}, u32[]{:S(2)}, u32[]{:S(2)}) async-start(bf16[4,25,65536]{2,1,0:T(8,128)(2,1)} %copy.25), calls=%async_computation | async-start | bytes 33554432 | tf_op jit(solution)/shard_map/all_to_all | solution.py:51
  99.9 568.3 %all-gather.2.cloned.1.call-start = ((), (), s32[]{:S(2)}) async-start(), calls=%async_computation.3 | async-start | bytes 16384000 | tf_op jit(solution)/shard_map/all_gather | solution.py:64
  105.0 603.0 %reduce-scatter.2.cloned.1.call-start = ((), (), s32[]{:S(2)}) async-start(), calls=%async_computation.4 | async-start | bytes 1310720 | tf_op jit(solution)/shard_map/reduce_scatter | solution.py:69
  668.3 14.7 %copy-start.6 = (f32[100]{0:T(128)S(1)}, f32[100]{0:T(128)}, u32[]{:S(2)}) copy-start(f32[100]{0:T(128)} %param.12) | copy-start | bytes 1204
  668.3 15.3 %copy-start.4 = (f32[512]{0:T(512)S(1)}, f32[512]{0:T(512)}, u32[]{:S(2)}) copy-start(f32[512]{0:T(512)} %param.13) | copy-start | bytes 6148
  668.3 41.8 %copy-start.1 = (s32[100,8]{0,1:T(8,128)S(1)}, s32[100,8]{0,1:T(8,128)}, u32[]{:S(2)}) copy-start(s32[100,8]{0,1:T(8,128)} %param.11) | copy-start | bytes 9604
Sparse Core Ops, SparseCore 0:
  105.2 86.2 all-gather.1
  683.0 25.0 reduce-scatter.1
where the time goes:
time: 723 us; the launch traced here: 717 us
  waiting for transfers between devices  380 us (53%)
  blocking collectives  194 us (27%)
  local copies, waits for them, and re-layouts  89.3 us (12%)
  other arithmetic  18.5 us (3%)
  matrix products  14.6 us (2%)
  between operations  13.5 us (2%)
  starting transfers between devices  7.31 us (1%)
    all_to_all x1, waiting for transfers between devices, on_device(): lax.all_to_all(packed, 'row', split_axis=0, concat_axis=0, tiled=True)  356 us
    all_to_all x1, blocking collectives, on_device(): lax.all_to_all(lax.all_to_all(packed, 'row', split_axis=0, concat_axis=0,...  194 us
    reshape x2, local copies, waits for them, and re-layouts, on_device(): amp_kept.reshape(batch_size, occ_share, vir_share, row_count, vir_share)  39.7 us
    reshape x2, local copies, waits for them, and re-layouts, on_device(): jnp.transpose(packed, (3, 1, 0, 4, 2))  32.4 us
    reduce_scatter x1, waiting for transfers between devices, on_device(): lax.psum_scatter(cycle_whole, 'row', scatter_dimension=0, tiled=True)  23.8 us
    dot_general x1, matrix products, on_device(): lax.dot_general(lax.all_gather(int_kept, 'col', axis=0, tiled=True), arra...  14.6 us
  transfers between devices with their start and end apart: 3, of which 2 were waited for; matrix products, arithmetic and copies ran while one was open for 3% of the time, Pallas kernels for 0%

commit v1 on v0

v1 whole, which is shorter than its diff:
```python
import jax
import jax.numpy as jnp
from jax import lax
from jax.sharding import PartitionSpec as P


def folded_integrals(integrals, occ_local, vir_local, vir_irrep, screen_rows, pair_label):
    half = vir_irrep.shape[0] // 2
    irrep_codes = jnp.arange(8, dtype=jnp.int32)
    screen_local = jnp.sum(
        screen_rows[:, None, :] * (vir_local[None, :, None] == irrep_codes).astype(jnp.int32),
        axis=2,
    )
    wanted = jnp.bitwise_xor(jnp.bitwise_xor(occ_local[:, None], vir_local[None, :]), pair_label)
    wanted = jnp.where(screen_local == 1, wanted, -1)[:, :, None]
    zeros = jnp.zeros((), integrals.dtype)
    low = jnp.where(wanted == vir_irrep[None, None, :half], integrals[:, :, :half], zeros)
    return jnp.where(wanted == vir_irrep[None, None, half:], integrals[:, :, half:], low)


def on_device(amplitudes, integrals, occ_irrep, vir_irrep, screen, occ_energy, vir_energy):
    row_count = lax.axis_size("row")
    column_count = lax.axis_size("col")
    row, col = lax.axis_index("row"), lax.axis_index("col")
    batch_size, occ_share, vir_share, vir_total = amplitudes.shape
    half = vir_total // 2
    vir_columns = vir_total // column_count
    occ_offset = col * occ_share
    occ_local = lax.dynamic_slice_in_dim(occ_irrep, occ_offset, occ_share)
    vir_local = lax.dynamic_slice_in_dim(vir_irrep, row * vir_share, vir_share)
    screen_rows = lax.dynamic_slice_in_dim(screen, occ_offset, occ_share, 0)
    pair_label = occ_irrep[batch_size]

    folded = folded_integrals(
        integrals, occ_local, vir_local, vir_irrep, screen_rows, pair_label
    )
    gathered = lax.all_gather(folded, "row", axis=1, tiled=True)
    shift = jnp.bitwise_xor(occ_irrep[:batch_size, None], occ_local[None, :])
    keep_amp = (
        jnp.bitwise_xor(shift[:, :, None], vir_local[None, None, :])[:, :, :, None]
        == vir_irrep[None, None, None, :]
    )
    amp_kept = jnp.where(keep_amp, amplitudes, jnp.zeros_like(amplitudes))
    partial = lax.dot_general(
        amp_kept, gathered, (((1, 3), (0, 1)), ((), ())), preferred_element_type=jnp.float32
    )

    if row_count == column_count and column_count == 4:
        piece = lax.psum_scatter(partial, "col", scatter_dimension=2, tiled=True)
        routes = []
        for flip in (0, 1):
            pairs = []
            for r in range(row_count):
                for q in range(column_count):
                    target = q // 2 + 2 * ((q + flip) % 2)
                    pairs.append((r * column_count + q, target * column_count + r))
            routes.append(lax.ppermute(piece, ("row", "col"), pairs))
        swap = row // 2 == 1
        first = jnp.where(swap, routes[1], routes[0])
        second = jnp.where(swap, routes[0], routes[1])
        cycle = jnp.concatenate([first, second], axis=2)
    else:
        whole = lax.all_gather(lax.psum(partial, "col"), "row", axis=1, tiled=True)
        cycle = lax.dynamic_slice_in_dim(whole, col * vir_columns, vir_columns, 1)
        cycle = lax.dynamic_slice_in_dim(cycle, (row * vir_share) % half, vir_share, 2)
    cycle = jnp.transpose(cycle, (2, 0, 1))
    col_irrep = lax.dynamic_slice_in_dim(vir_irrep, col * vir_columns, vir_columns)
    kept = (
        jnp.bitwise_xor(occ_irrep[:batch_size, None], pair_label ^ col_irrep[None, :])[None]
        == vir_local[:, None, None]
    )
    cycle = jnp.where(kept, cycle, 0.0)
    energy_cols = lax.dynamic_slice_in_dim(vir_energy, col * vir_columns, vir_columns)
    energy_rows = lax.dynamic_slice_in_dim(vir_energy, row * vir_share, vir_share)
    denominator = (
        occ_energy[:batch_size][None, :, None]
        + occ_energy[batch_size]
        - energy_cols[None, None, :]
        - energy_rows[:, None, None]
    )
    return cycle / denominator


def solution(mesh):
    in_specs = (
        P("parts", "col", "row", None),
        P(("parts", "col"), "row", None),
        P("parts"),
        P("parts"),
        P("parts", None),
        P("parts"),
        P("parts"),
    )
    out_specs = P("row", "parts", "col")
    return jax.shard_map(
        on_device, mesh=mesh, in_specs=in_specs, out_specs=out_specs, check_vma=False
    )
```

time: 723 us -> 193 us (0.27)
  waiting for transfers between devices: 380 us -> 134 us
  blocking collectives: 194 us -> 0 us
  local copies, waits for them, and re-layouts: 89.3 us -> 13.1 us
    all_to_all x1 -> x0, waiting for transfers between devices: 356 us -> none  [on_device(): lax.all_to_all(packed, 'row', split_axis=0, concat_axis=0, tiled=True)]
    all_to_all x1 -> x0, blocking collectives: 194 us -> none  [on_device(): lax.all_to_all(lax.all_to_all(packed, 'row', split_axis=0, concat_axis=0,...]
    all_gather x1, waiting for transfers between devices: 0.01 us -> 106 us  [on_device(): gathered = lax.all_gather(folded, 'row', axis=1, tiled=True)]
    reshape x5 -> x0, local copies, waits for them, and re-layouts: 85.5 us -> none  [the longest x2 39.7 us: on_device(): amp_kept.reshape(batch_size, occ_share, vir_share, row_count, vir_share)]
    select_n x2 -> x3, other arithmetic: 14.4 us -> 2.79 us  [the longest x1 2.05 us: folded_integrals(): jnp.where(wanted == vir_irrep[None, None, half:], integrals[:, :, half:],...]
    dot_general x0 -> x1, other arithmetic: none -> 10.7 us  [on_device(): lax.dot_general(amp_kept, gathered, (((1, 3), (0, 1)), ((), ())), preferr...]
  transfers between devices with their start and end apart: 3 -> 4, of which waited for: 2 -> 4; matrix products, arithmetic and copies ran while one was open for 3% -> 6% of each run, Pallas kernels for 0% -> 0%
where the time goes in v1:
time: 193 us; the launch traced here: 190 us
  waiting for transfers between devices  134 us (69%)
  other arithmetic  16.1 us (8%)
  between operations  13.5 us (7%)
  local copies, waits for them, and re-layouts  13.1 us (7%)
  matrix products  9.21 us (5%)
  starting transfers between devices  4.54 us (2%)
    all_gather x1, waiting for transfers between devices, on_device(): gathered = lax.all_gather(folded, 'row', axis=1, tiled=True)  106 us
    reduce_scatter x1, waiting for transfers between devices, on_device(): piece = lax.psum_scatter(partial, 'col', scatter_dimension=2, tiled=True)  21.5 us
    dot_general x1, other arithmetic, on_device(): lax.dot_general(amp_kept, gathered, (((1, 3), (0, 1)), ((), ())), preferr...  10.7 us
    dot_general x1, matrix products, on_device(): lax.dot_general(amp_kept, gathered, (((1, 3), (0, 1)), ((), ())), preferr...  9.21 us
    ppermute x2, waiting for transfers between devices, on_device(): routes.append(lax.ppermute(piece, ('row', 'col'), pairs))  5.83 us
    unnamed x12, local copies, waits for them, and re-layouts  5.25 us
    ppermute x2, starting transfers between devices, on_device(): routes.append(lax.ppermute(piece, ('row', 'col'), pairs))  4.49 us
  transfers between devices with their start and end apart: 4, of which 4 were waited for; matrix products, arithmetic and copies ran while one was open for 6% of the time, Pallas kernels for 0%

profile of v1, /device:TPU:24, one launch (start us, length us, event | category | flops | bytes accessed | tf_op | source)
XLA Modules:
  0.0 190.3 jit_solution(17666716235107848208)
XLA Ops:
  6.5 0.0 copy-start
  6.5 0.0 all-gather.2.cloned.1.call-start
  6.5 1.2 slice.26
  7.8 0.8 fusion.14
  8.5 1.5 dynamic-slice_xor_fusion
  10.0 0.7 dynamic_slice.20
  10.8 0.0 copy-done
  10.8 0.1 constant_dynamic-slice_fusion
  10.8 0.1 copy.12
  10.9 3.4 %fusion.12 = (bf16[25,128,256]{2,1,0:T(8,128)(2,1)}, bf16[25,128,256]{2,1,0:T(8,128)(2,1)S(1)}) fusion(bf16[25,128,512]{2,1,0:T(8,128)(2,1)} %param.8), kind=kLoop, calls=%fused_computation.26 | loop fusion | bytes 6553600 | tf_op jit(solution)/shard_map/slice | solution.py:17
  14.4 2.1 %copy.17 = bf16[25,128,256]{1,2,0:T(8,128)(2,1)S(1)} copy(bf16[25,128,256]{2,1,0:T(8,128)(2,1)S(1)} %get-tuple-element.6) | data formatting | bytes 3276800
  16.5 3.1 %copy.18 = bf16[25,128,256]{1,2,0:T(8,128)(2,1)S(1)} copy(bf16[25,128,256]{2,1,0:T(8,128)(2,1)} %get-tuple-element.5) | data formatting | bytes 3276800
  19.6 0.1 multiply_reduce_fusion
  19.7 0.7 xor_select_fusion
  20.4 0.0 copy-start.2
  20.4 0.0 copy-start.1
  20.4 2.1 %compare_select_fusion.3 = bf16[25,128,256]{1,2,0:T(8,128)(2,1)} fusion(bf16[25,128,256]{1,2,0:T(8,128)(2,1)S(1)} %copy.17, bf16[25,128,256]{1,2,0:T(8,128)(2,1)S(1)} %copy.18, s32[25,128]{1,0:T(8,128)S(1)} %xor_select_fusion, s32[256]{0:T(256)S(1)} %get-tuple-element.14, s32[256]{0:T(256)S(1)} %get-tuple-element.13), kind=kLoop, calls=%fused_computation.7 | loop fusion | flops 3276800 | bytes 4930048 | tf_op jit(solution)/shard_map/jit(_where)/select_n | solution.py:18
  22.5 0.0 all-gather.2.cloned.1.call-update
  22.5 0.0 reduce-scatter.2.cloned.1.call-start
  22.6 0.0 copy-done.2
  22.6 0.1 broadcast_xor_fusion.1
  22.6 0.1 broadcast_xor_fusion
  22.7 0.0 copy-done.1
  22.7 10.7 %compare_select_fusion.8 = bf16[4,25,128,512]{3,2,1,0:T(8,128)(2,1)} fusion(bf16[4,25,128,512]{3,2,1,0:T(8,128)(2,1)} %param.7, s32[512]{0:T(512)S(1)} %copy-done.1, s32[4,25,128]{2,1,0:T(8,128)S(1)} %broadcast_xor_fusion), kind=kLoop, calls=%fused_computation.clone.clone.clone.clone.1 | loop fusion | flops 13107200 | bytes 26267648 | tf_op jit(solution)/shard_map/dot_general | solution.py:44
  33.4 0.0 copy-start.4
  33.4 0.0 copy-start.3
  33.5 106.5 %all-gather.2.cloned.1.call-done = bf16[25,512,256]{1,2,0:T(8,128)(2,1)} async-done(((bf16[25,128,256]{1,2,0:T(8,128)(2,1)}), bf16[25,512,256]{1,2,0:T(8,128)(2,1)}) %all-gather.2.cloned.1.call-update) | async-done | bytes 6553616 | tf_op jit(solution)/shard_map/all_gather | solution.py:37
  139.9 9.2 %fusion.5 = f32[4,128,256]{1,2,0:T(8,128)} fusion(bf16[25,512,256]{1,2,0:T(8,128)(2,1)} %all-gather.2.cloned.1.call-done, bf16[4,25,128,512]{3,2,1,0:T(8,128)(2,1)} %compare_select_fusion.8), kind=kOutput, calls=%fused_computation.8 | convolution fusion | flops 3355443200 | bytes 20185088 | tf_op jit(solution)/shard_map/dot_general | solution.py:44
  149.1 0.0 reduce-scatter.2.cloned.1.call-update
  149.2 0.0 copy-done.4
  149.2 0.6 slice.32
  149.8 0.0 copy-done.3
  149.8 0.1 fusion.13
  149.8 0.6 slice_add_fusion
  150.5 0.1 broadcast_xor_fusion.2
  150.6 21.5 %reduce-scatter.2.cloned.1.call-done = f32[4,128,64]{1,2,0:T(8,128)} async-done(((f32[4,128,256]{1,2,0:T(8,128)}), f32[4,128,64]{1,2,0:T(8,128)}) %reduce-scatter.2.cloned.1.call-update) | async-done | bytes 131088 | tf_op jit(solution)/shard_map/reduce_scatter | solution.py:49
  172.0 0.0 collective-permute-start
  172.0 4.5 %collective-permute-start.1 = (f32[4,128,64]{1,2,0:T(8,128)}, f32[4,128,64]{1,2,0:T(8,128)S(1)}, u32[]{:S(2)}, u32[]{:S(2)}) collective-permute-start(f32[4,128,64]{1,2,0:T(8,128)} %reduce-scatter.2.cloned.1.call-done), channel_id=1, source_target_pairs={{0,0},{1,8},{2,4},{3,12},{4,1},{5,9},{6,5},{7,13},{8,2},{9,10},{10... | collective-permute-start | bytes 393224 | tf_op jit(solution)/shard_map/ppermute | solution.py:57
  176.5 0.1 broadcast_subtract_fusion
  176.6 3.6 %collective-permute-done = f32[4,128,64]{1,2,0:T(8,128)S(1)} collective-permute-done((f32[4,128,64]{1,2,0:T(8,128)}, f32[4,128,64]{1,2,0:T(8,128)S(1)}, u32[]{:S(2)}, u32[]{:S(2)}) %collective-permute-start) | collective-permute-done | bytes 131104 | tf_op jit(solution)/shard_map/ppermute | solution.py:57
  180.2 2.3 %collective-permute-done.1 = f32[4,128,64]{1,2,0:T(8,128)S(1)} collective-permute-done((f32[4,128,64]{1,2,0:T(8,128)}, f32[4,128,64]{1,2,0:T(8,128)S(1)}, u32[]{:S(2)}, u32[]{:S(2)}) %collective-permute-start.1) | collective-permute-done | bytes 131104 | tf_op jit(solution)/shard_map/ppermute | solution.py:57
  182.4 0.1 fusion.9
  182.6 0.9 copy.15
  (2 shorter events, 0.0 us)
Async XLA Ops:
  6.5 4.2 %copy-start = (s32[100,8]{0,1:T(8,128)S(1)}, s32[100,8]{0,1:T(8,128)}, u32[]{:S(2)}) copy-start(s32[100,8]{0,1:T(8,128)} %param.11) | copy-start | bytes 9604
  6.5 133.4 %all-gather.2.cloned.1.call-start = ((), (), s32[]{:S(2)}) async-start(), calls=%async_computation.1 | async-start | bytes 8192000 | tf_op jit(solution)/shard_map/all_gather | solution.py:37
  20.4 2.1 %copy-start.2 = (s32[100]{0:T(128)S(1)}, s32[100]{0:T(128)}, u32[]{:S(2)}) copy-start(s32[100]{0:T(128)} %param.9) | copy-start | bytes 1204
  20.4 2.3 %copy-start.1 = (s32[512]{0:T(512)S(1)}, s32[512]{0:T(512)}, u32[]{:S(2)}) copy-start(s32[512]{0:T(512)} %param.10) | copy-start | bytes 6148
  22.5 149.5 %reduce-scatter.2.cloned.1.call-start = ((), (), s32[]{:S(2)}) async-start(), calls=%async_computation.2 | async-start | bytes 655360 | tf_op jit(solution)/shard_map/reduce_scatter | solution.py:49
  33.4 115.7 %copy-start.4 = (f32[100]{0:T(128)S(1)}, f32[100]{0:T(128)}, u32[]{:S(2)}) copy-start(f32[100]{0:T(128)} %param.12) | copy-start | bytes 1204
  33.4 116.3 %copy-start.3 = (f32[512]{0:T(512)S(1)}, f32[512]{0:T(512)}, u32[]{:S(2)}) copy-start(f32[512]{0:T(512)} %param.13) | copy-start | bytes 6148
  172.0 8.1 %collective-permute-start = (f32[4,128,64]{1,2,0:T(8,128)}, f32[4,128,64]{1,2,0:T(8,128)S(1)}, u32[]{:S(2)}, u32[]{:S(2)}) collective-permute-start(f32[4,128,64]{1,2,0:T(8,128)} %reduce-scatter.2.cloned.1.call-done), channel_id=1, source_target_pairs={{0,8},{1,0},{2,12},{3,4},{4,9},{5,1},{6,13},{7,5},{8,10},{9,2},{10... | collective-permute-start | bytes 393224 | tf_op jit(solution)/shard_map/ppermute | solution.py:57
  172.0 10.4 %collective-permute-start.1 = (f32[4,128,64]{1,2,0:T(8,128)}, f32[4,128,64]{1,2,0:T(8,128)S(1)}, u32[]{:S(2)}, u32[]{:S(2)}) collective-permute-start(f32[4,128,64]{1,2,0:T(8,128)} %reduce-scatter.2.cloned.1.call-done), channel_id=1, source_target_pairs={{0,0},{1,8},{2,4},{3,12},{4,1},{5,9},{6,5},{7,13},{8,2},{9,10},{10... | collective-permute-start | bytes 393224 | tf_op jit(solution)/shard_map/ppermute | solution.py:57
Sparse Core Ops, SparseCore 0:
  22.6 117.2 all-gather.1
  149.3 22.6 reduce-scatter.1

commit v2 on v1

--- a/solution.py
+++ b/solution.py
@@ -1,7 +1,15 @@
+import functools
+
 import jax
 import jax.numpy as jnp
 from jax import lax
+from jax.experimental import pallas as pl
+from jax.experimental.pallas import tpu as pltpu
 from jax.sharding import PartitionSpec as P
+
+LANES = 128
+SIDE = 4
+PIECES = 5
 
 
 def folded_integrals(integrals, occ_local, vir_local, vir_irrep, screen_rows, pair_label):
@@ -16,6 +24,332 @@
     zeros = jnp.zeros((), integrals.dtype)
     low = jnp.where(wanted == vir_irrep[None, None, :half], integrals[:, :, :half], zeros)
     return jnp.where(wanted == vir_irrep[None, None, half:], integrals[:, :, half:], low)
+
+
+def cycle_kernel(
+    step,
+    occ_ref,
+    screen_ref,
+    label_rows_ref,
+    label_cols_ref,
+    int_hbm,
+    amp_hbm,
+    out_ref,
+    raw,
+    amp,
+    mask,
+    one_hot,
+    shards,
+    total,
+    from_cols,
+    halves,
+    landed,
+    raw_sem,
+    amp_sem,
+    send_sem,
+    recv_sem,
+    col_send,
+    col_recv,
+    end_send,
+    end_recv,
+):
+    part, row, col = lax.axis_index("parts"), lax.axis_index("row"), lax.axis_index("col")
+    batch_size = amp.shape[1]
+    occ_share = raw.shape[0]
+    first_k = col * occ_share
+
+    def remote(source, target, send, recv, to_row, to_col):
+        return pltpu.make_async_remote_copy(
+            src_ref=source,
+            dst_ref=target,
+            send_sem=send,
+            recv_sem=recv,
+            device_id=(part, to_row, to_col),
+            device_id_type=pl.DeviceIdType.MESH,
+        )
+
+    raw_copies = []
+    for j in range(PIECES):
+        span = pl.ds(j * step, step)
+        copy = pltpu.make_async_copy(int_hbm.at[span], raw.at[span], raw_sem.at[j])
+        copy.start()
+        raw_copies.append(copy)
+    amp_copies = []
+    for c in range(SIDE):
+        copy = pltpu.make_async_copy(
+            amp_hbm.at[:, :, :, pl.ds(c * LANES, LANES)], amp.at[c], amp_sem.at[c]
+        )
+        copy.start()
+        amp_copies.append(copy)
+
+    barrier = pltpu.get_barrier_semaphore()
+    for ahead_row in range(SIDE):
+        for ahead_col in range(SIDE):
+            if ahead_row or ahead_col:
+                pl.semaphore_signal(
+                    barrier,
+                    inc=1,
+                    device_id=(
+                        part,
+                        lax.rem(row + ahead_row, SIDE),
+                        lax.rem(col + ahead_col, SIDE),
+                    ),
+                    device_id_type=pl.DeviceIdType.MESH,
+                )
+
+    row_label = label_cols_ref[...]
+    for c in range(SIDE):
+        differ = jnp.bitwise_xor(row_label, label_rows_ref[c : c + 1, :])
+        for m in range(8):
+            mask[c, m] = jnp.where(differ == m, 1.0, 0.0).astype(mask.dtype)
+    for m in range(8):
+        one_hot[m] = jnp.where(row_label == m, 1.0, 0.0)
+    total[...] = jnp.zeros_like(total)
+
+    def fold(k, carry):
+        shift = jnp.bitwise_xor(occ_ref[first_k + k], occ_ref[batch_size])
+        screened = jnp.zeros((LANES, LANES), jnp.float32)
+        for m in range(8):
+            screened += screen_ref[(first_k + k) * 8 + m].astype(jnp.float32) * one_hot[m]
+        screened = screened.astype(raw.dtype)
+        for h in range(SIDE // 2):
+            low = raw[k, :, h * LANES : (h + 1) * LANES] * mask[h, shift]
+            g = h + SIDE // 2
+            high = raw[k, :, g * LANES : (g + 1) * LANES] * mask[g, shift]
+            shards[row, k, :, h * LANES : (h + 1) * LANES] = (low + high) * screened
+        return carry
+
+    def hop(distance, j, up):
+        way = 0 if up else 1
+        owner = row - distance if up else row + distance
+        piece = shards.at[owner, pl.ds(j * step, step)]
+        return remote(
+            piece,
+            piece,
+            send_sem.at[way, distance, j],
+            recv_sem.at[way, distance, j],
+            row + 1 if up else row - 1,
+            col,
+        )
+
+    def arrival(distance, j, up):
+        way = 0 if up else 1
+        owner = row - distance if up else row + distance
+        piece = shards.at[owner, pl.ds(j * step, step)]
+        return remote(
+            piece,
+            piece,
+            send_sem.at[way, distance - 1, j],
+            recv_sem.at[way, distance - 1, j],
+            row - 1 if up else row + 1,
+            col,
+        )
+
+    def accumulate(owner, j):
+        def one(t, carry):
+            k = j * step + t
+            rows = []
+            for i in range(batch_size):
+                shift = jnp.bitwise_xor(occ_ref[i], occ_ref[first_k + k])
+                rows.append(amp[owner, i, k] * mask[owner, shift])
+            total[...] += jnp.dot(
+                jnp.concatenate(rows, axis=0),
+                shards[owner, k],
+                preferred_element_type=jnp.float32,
+            )
+            return carry
+
+        lax.fori_loop(0, step, one, 0)
+
+    for j in range(PIECES):
+        raw_copies[j].wait()
+        lax.fori_loop(j * step, (j + 1) * step, fold, 0)
+        if j == 0:
+            pl.semaphore_wait(barrier, SIDE * SIDE - 1)
+
+        @pl.when(row < SIDE - 1)
+        def _():
+            hop(0, j, True).start()
+
+        @pl.when(row > 0)
+        def _():
+            hop(0, j, False).start()
+
+    for copy in amp_copies:
+        copy.wait()
+    for j in range(PIECES):
+        accumulate(row, j)
+
+    for distance in range(1, SIDE):
+        for j in range(PIECES):
+
+            @pl.when(row >= distance)
+            def _():
+                arrival(distance, j, True).wait_recv()
+                if distance < SIDE - 1:
+
+                    @pl.when(row < SIDE - 1)
+                    def _():
+                        hop(distance, j, True).start()
+
+            @pl.when(row + distance < SIDE)
+            def _():
+                arrival(distance, j, False).wait_recv()
+                if distance < SIDE - 1:
+
+                    @pl.when(row > 0)
+                    def _():
+                        hop(distance, j, False).start()
+
+            @pl.when(row >= distance)
+            def _():
+                accumulate(row - distance, j)
+
+            @pl.when(row + distance < SIDE)
+            def _():
+                accumulate(row + distance, j)
+
+    share = total.shape[0] // SIDE
+    col_copies = []
+    for ahead in range(1, SIDE):
+        to_col = lax.rem(col + ahead, SIDE)
+        copy = remote(
+            total.at[pl.ds(pl.multiple_of(to_col * share, share), share)],
+            from_cols.at[ahead - 1],
+            col_send.at[ahead - 1],
+            col_recv.at[ahead - 1],
+            row,
+            to_col,
+        )
+        copy.start()
+        col_copies.append(copy)
+    summed = total[pl.ds(pl.multiple_of(col * share, share), share), :]
+    for ahead in range(1, SIDE):
+        col_copies[ahead - 1].wait_recv()
+        summed += from_cols[ahead - 1]
+    halves[0] = summed[:, :LANES]
+    halves[1] = summed[:, LANES:]
+
+    def deliver(ahead):
+        to_row = lax.rem(row + ahead, SIDE)
+        return remote(
+            halves.at[lax.rem(to_row, 2)],
+            landed.at[col],
+            end_send.at[ahead],
+            end_recv.at[col],
+            to_row,
+            row,
+        )
+
+    for ahead in range(1, SIDE):
+        deliver(ahead).start()
+
+    @pl.when(row != col)
+    def _():
+        deliver(0).start()
+
+    @pl.when(row == col)
+    def _():
+        landed[col] = halves[lax.rem(row, 2)]
+
+    def delivered(i):
+        return remote(
+            halves.at[0],
+            landed.at[i],
+            end_send.at[0],
+            end_recv.at[i],
+            lax.rem(row + 1, SIDE),
+            col,
+        )
+
+    for i in range(SIDE):
+
+        @pl.when((row != col) | (col != i))
+        def _():
+            delivered(i).wait_recv()
+
+        out_ref[i] = landed[i]
+
+    for ahead in range(1, SIDE):
+        col_copies[ahead - 1].wait_send()
+        deliver(ahead).wait_send()
+
+    @pl.when(row != col)
+    def _():
+        deliver(0).wait_send()
+
+    for distance in range(SIDE - 1):
+        for j in range(PIECES):
+
+            @pl.when((row >= distance) & (row < SIDE - 1))
+            def _():
+                hop(distance, j, True).wait_send()
+
+            @pl.when((row + distance < SIDE) & (row > 0))
+            def _():
+                hop(distance, j, False).wait_send()
+
+
+def cycle_blocks(amplitudes, integrals, occ_irrep, vir_irrep, vir_local, screen):
+    batch_size, occ_share, vir_share, vir_total = amplitudes.shape
+    half = vir_total // 2
+    bf16, f32 = jnp.bfloat16, jnp.float32
+    step = occ_share // PIECES
+    vmem, smem = pltpu.VMEM, pltpu.SMEM
+    hops = (2, SIDE - 1, PIECES)
+    return pl.pallas_call(
+        functools.partial(cycle_kernel, step),
+        out_shape=jax.ShapeDtypeStruct((batch_size, LANES, LANES), f32),
+        in_specs=[
+            pl.BlockSpec(memory_space=smem),
+            pl.BlockSpec(memory_space=smem),
+            pl.BlockSpec(memory_space=vmem),
+            pl.BlockSpec(memory_space=vmem),
+            pl.BlockSpec(memory_space=pl.ANY),
+            pl.BlockSpec(memory_space=pl.ANY),
+        ],
+        out_specs=pl.BlockSpec(memory_space=vmem),
+        scratch_shapes=[
+            vmem((occ_share, vir_share, vir_total), bf16),
+            vmem((SIDE, batch_size, occ_share, vir_share, LANES), bf16),
+            vmem((SIDE, 8, vir_share, LANES), bf16),
+            vmem((8, vir_share, LANES), f32),
+            vmem((SIDE, occ_share, vir_share, half), bf16),
+            vmem((batch_size * vir_share, half), f32),
+            vmem((SIDE - 1, vir_share, half), f32),
+            vmem((2, vir_share, LANES), f32),
+            vmem((SIDE, vir_share, LANES), f32),
+            pltpu.SemaphoreType.DMA((PIECES,)),
+            pltpu.SemaphoreType.DMA((SIDE,)),
+            pltpu.SemaphoreType.DMA(hops),
+            pltpu.SemaphoreType.DMA(hops),
+            pltpu.SemaphoreType.DMA((SIDE - 1,)),
+            pltpu.SemaphoreType.DMA((SIDE - 1,)),
+            pltpu.SemaphoreType.DMA((SIDE,)),
+            pltpu.SemaphoreType.DMA((SIDE,)),
+        ],
+        compiler_params=pltpu.CompilerParams(
+            collective_id=0, has_side_effects=True, vmem_limit_bytes=48 * 1024 * 1024
+        ),
+        name="cycle_blocks",
+    )(
+        occ_irrep,
+        screen.reshape(-1),
+        vir_irrep.reshape(SIDE, LANES),
+        jnp.broadcast_to(vir_local[:, None], (vir_share, LANES)),
+        integrals,
+        amplitudes,
+    )
+
+
+def fits_kernel(row_count, column_count, amplitudes):
+    batch_size, occ_share, vir_share, vir_total = amplitudes.shape
+    return (
+        row_count == column_count == batch_size == SIDE
+        and vir_share == LANES
+        and vir_total == SIDE * LANES
+        and occ_share % PIECES == 0
+    )
 
 
 def on_device(amplitudes, integrals, occ_irrep, vir_irrep, screen, occ_energy, vir_energy):
@@ -31,35 +365,22 @@
     screen_rows = lax.dynamic_slice_in_dim(screen, occ_offset, occ_share, 0)
     pair_label = occ_irrep[batch_size]
 
-    folded = folded_integrals(
-        integrals, occ_local, vir_local, vir_irrep, screen_rows, pair_label
-    )
-    gathered = lax.all_gather(folded, "row", axis=1, tiled=True)
-    shift = jnp.bitwise_xor(occ_irrep[:batch_size, None], occ_local[None, :])
-    keep_amp = (
-        jnp.bitwise_xor(shift[:, :, None], vir_local[None, None, :])[:, :, :, None]
-        == vir_irrep[None, None, None, :]
-    )
-    amp_kept = jnp.where(keep_amp, amplitudes, jnp.zeros_like(amplitudes))
-    partial = lax.dot_general(
-        amp_kept, gathered, (((1, 3), (0, 1)), ((), ())), preferred_element_type=jnp.float32
-    )
-
-    if row_count == column_count and column_count == 4:
-        piece = lax.psum_scatter(partial, "col", scatter_dimension=2, tiled=True)
-        routes = []
-        for flip in (0, 1):
-            pairs = []
-            for r in range(row_count):
-                for q in range(column_count):
-                    target = q // 2 + 2 * ((q + flip) % 2)
-                    pairs.append((r * column_count + q, target * column_count + r))
-            routes.append(lax.ppermute(piece, ("row", "col"), pairs))
-        swap = row // 2 == 1
-        first = jnp.where(swap, routes[1], routes[0])
-        second = jnp.where(swap, routes[0], routes[1])
-        cycle = jnp.concatenate([first, second], axis=2)
+    if fits_kernel(row_count, column_count, amplitudes):
+        cycle = cycle_blocks(amplitudes, integrals, occ_irrep, vir_irrep, vir_local, screen)
     else:
+        folded = folded_integrals(
+            integrals, occ_local, vir_local, vir_irrep, screen_rows, pair_label
+        )
+        gathered = lax.all_gather(folded, "row", axis=1, tiled=True)
+        shift = jnp.bitwise_xor(occ_irrep[:batch_size, None], occ_local[None, :])
+        keep_amp = (
+            jnp.bitwise_xor(shift[:, :, None], vir_local[None, None, :])[:, :, :, None]
+            == vir_irrep[None, None, None, :]
+        )
+        amp_kept = jnp.where(keep_amp, amplitudes, jnp.zeros_like(amplitudes))
+        partial = lax.dot_general(
+            amp_kept, gathered, (((1, 3), (0, 1)), ((), ())), preferred_element_type=jnp.float32
+        )
         whole = lax.all_gather(lax.psum(partial, "col"), "row", axis=1, tiled=True)
         cycle = lax.dynamic_slice_in_dim(whole, col * vir_columns, vir_columns, 1)
         cycle = lax.dynamic_slice_in_dim(cycle, (row * vir_share) % half, vir_share, 2)

time: 193 us -> 141 us (0.73); the launches traced: 190 us -> 141 us
  waiting for transfers between devices: 134 us -> 0 us
  Pallas kernels: 0 us -> 129 us
  between operations: 13.5 us -> 0.03 us
  other arithmetic: 16.1 us -> 3.75 us
  matrix products: 9.21 us -> 0 us
  local copies, waits for them, and re-layouts: 13.1 us -> 8.37 us
  starting transfers between devices: 4.54 us -> 0 us
    pallas_call x0 -> x1, Pallas kernels: none -> 129 us  [cycle_blocks(): pl.pallas_call(functools.partial(cycle_kernel, step), out_shape=jax.Shape...]
    all_gather x1 -> x0, waiting for transfers between devices: 106 us -> none  [on_device(): gathered = lax.all_gather(folded, 'row', axis=1, tiled=True)]
    reduce_scatter x1 -> x0, waiting for transfers between devices: 21.5 us -> none  [on_device(): piece = lax.psum_scatter(partial, 'col', scatter_dimension=2, tiled=True)]
    dot_general x1 -> x0, other arithmetic: 10.7 us -> none  [on_device(): lax.dot_general(amp_kept, gathered, (((1, 3), (0, 1)), ((), ())), preferr...]
    dot_general x1 -> x0, matrix products: 9.21 us -> none  [on_device(): lax.dot_general(amp_kept, gathered, (((1, 3), (0, 1)), ((), ())), preferr...]
    ppermute x2 -> x0, waiting for transfers between devices: 5.83 us -> none  [on_device(): routes.append(lax.ppermute(piece, ('row', 'col'), pairs))]
    ppermute x2 -> x0, starting transfers between devices: 4.49 us -> none  [on_device(): routes.append(lax.ppermute(piece, ('row', 'col'), pairs))]
    slice x2 -> x0, local copies, waits for them, and re-layouts: 4.18 us -> none  [the longest x1 3.42 us: folded_integrals(): integrals[:, :, :half]]
  transfers between devices with their start and end apart: 4 -> 0, of which waited for: 4 -> 0; matrix products, arithmetic and copies ran while one was open for 6% -> 0% of each run, Pallas kernels for 0% -> 0%
where the time goes in v2:
time: 141 us
  Pallas kernels  129 us (91%)
  local copies, waits for them, and re-layouts  8.37 us (6%)
  other arithmetic  3.75 us (3%)
    pallas_call x1, Pallas kernels, cycle_blocks(): pl.pallas_call(functools.partial(cycle_kernel, step), out_shape=jax.Shape...  129 us
    unnamed x7, local copies, waits for them, and re-layouts  4.06 us

profile of v2, /device:TPU:24, one launch (start us, length us, event | category | flops | bytes accessed | tf_op | source)
XLA Modules:
  0.0 140.7 jit_solution(16335862425379118400)
XLA Ops:
  0.0 1.2 slice.13
  1.2 1.2 slice.15
  2.5 1.3 slice_add_fusion
  3.8 1.5 %dynamic-slice_xor_fusion = (s32[128]{0:T(128)S(1)}, s32[128]{0:T(128)S(1)}) fusion(s32[512]{0:T(512)} %param.10, s32[]{:T(128)S(6)} %select_n.12, s32[]{:T(128)} %bitcast, s32[]{:T(128)S(6)} %select_n.13), kind=kLoop, calls=%fused_computation.5 | loop fusion | flops 128 | bytes 2060 | tf_op jit(solution)/shard_map/xor | solution.py:390
  5.2 0.8 fusion.1
  6.1 0.1 broadcast_subtract_fusion
  6.1 0.7 broadcast_xor_fusion
  6.9 0.8 copy.9
  7.7 0.1 reshape.70.screen_ref
  7.7 0.1 broadcast_in_dim.5.label_cols_ref
  7.8 0.0 copy-start
  7.8 1.9 %copy-done = bf16[25,128,512]{2,1,0:T(8,128)(2,1)S(1)} copy-done((bf16[25,128,512]{2,1,0:T(8,128)(2,1)S(1)}, bf16[25,128,512]{2,1,0:T(8,128)(2,1)}, u32[]{:S(2)}) %copy-start) | copy-done | bytes 3276824
  9.8 0.0 copy-start.1
  9.8 0.7 copy-done.1
  10.4 0.0 copy-start.2
  10.4 0.7 copy-done.2
  11.1 128.6 %cycle_blocks.1 = f32[4,128,128]{2,1,0:T(8,128)S(1)} custom-call(s32[100]{0:T(128)S(1)} %copy-done.2, s32[800]{0:T(1024)S(1)} %reshape.70.screen_ref, s32[4,128]{1,0:T(4,128)S(1)} %bitcast.8, s32[128,128]{1,0:T(8,128)S(1)} %broadcast_in_dim.5.label_cols_ref, bf16[25,128,512]{2,1,0:T(8,128)(2,1)S(1)} %copy-done, bf16[4,25,128,512]{3,2,1,0:T(8,128)(2,1)} %amp_hbm.1), custom_call_target="tpu_custom_call" | custom-call | tf_op jit(solution)/shard_map/cycle_blocks/pallas_call | solution.py:300
  139.7 0.2 fusion
  139.9 0.8 copy.10
Async XLA Ops:
  7.8 1.9 %copy-start = (bf16[25,128,512]{2,1,0:T(8,128)(2,1)S(1)}, bf16[25,128,512]{2,1,0:T(8,128)(2,1)}, u32[]{:S(2)}) copy-start(bf16[25,128,512]{2,1,0:T(8,128)(2,1)} %int_hbm.1) | copy-start | bytes 9830404
  9.8 0.7 copy-start.1
  10.4 0.7 copy-start.2

commit v3 on v2

--- a/solution.py
+++ b/solution.py
@@ -9,7 +9,9 @@
 
 LANES = 128
 SIDE = 4
-PIECES = 5
+GIVEN = (4, 3)
+OWN = 3
+PIECES = len(GIVEN) + OWN
 
 
 def folded_integrals(integrals, occ_local, vir_local, vir_irrep, screen_rows, pair_label):
@@ -27,11 +29,12 @@
 
 
 def cycle_kernel(
-    step,
+    sizes,
     occ_ref,
     screen_ref,
+    occ_energy_ref,
     label_rows_ref,
-    label_cols_ref,
+    energy_rows_ref,
     int_hbm,
     amp_hbm,
     out_ref,
@@ -44,6 +47,13 @@
     from_cols,
     halves,
     landed,
+    end_mask,
+    amp_out,
+    amp_in,
+    end_total,
+    end_cols,
+    end_sum,
+    from_inner,
     raw_sem,
     amp_sem,
     send_sem,
@@ -52,11 +62,29 @@
     col_recv,
     end_send,
     end_recv,
+    give_send,
+    give_recv,
+    give_col_send,
+    give_col_recv,
+    back_send,
+    back_recv,
 ):
     part, row, col = lax.axis_index("parts"), lax.axis_index("row"), lax.axis_index("col")
     batch_size = amp.shape[1]
     occ_share = raw.shape[0]
     first_k = col * occ_share
+    is_end = (row == 0) | (row == SIDE - 1)
+    is_inner = (row > 0) & (row < SIDE - 1)
+    upper = row // (SIDE // 2)
+    end_row = upper * (SIDE - 1)
+    inner_row = 1 + upper * (SIDE - 3)
+    starts = [sum(sizes[:j]) for j in range(PIECES + 1)]
+
+    def span_of(j):
+        return pl.ds(starts[j], sizes[j])
+
+    def column_of(ref, which):
+        return jnp.broadcast_to(ref[pl.ds(which, 1), :], (LANES, LANES)).T
 
     def remote(source, target, send, recv, to_row, to_col):
         return pltpu.make_async_remote_copy(
@@ -70,7 +98,7 @@
 
     raw_copies = []
     for j in range(PIECES):
-        span = pl.ds(j * step, step)
+        span = span_of(j)
         copy = pltpu.make_async_copy(int_hbm.at[span], raw.at[span], raw_sem.at[j])
         copy.start()
         raw_copies.append(copy)
@@ -97,7 +125,7 @@
                     device_id_type=pl.DeviceIdType.MESH,
                 )
 
-    row_label = label_cols_ref[...]
+    row_label = column_of(label_rows_ref, row)
     for c in range(SIDE):
         differ = jnp.bitwise_xor(row_label, label_rows_ref[c : c + 1, :])
         for m in range(8):
@@ -110,7 +138,7 @@
         shift = jnp.bitwise_xor(occ_ref[first_k + k], occ_ref[batch_size])
         screened = jnp.zeros((LANES, LANES), jnp.float32)
         for m in range(8):
-            screened += screen_ref[(first_k + k) * 8 + m].astype(jnp.float32) * one_hot[m]
+            screened += screen_ref[first_k + k, m].astype(jnp.float32) * one_hot[m]
         screened = screened.astype(raw.dtype)
         for h in range(SIDE // 2):
             low = raw[k, :, h * LANES : (h + 1) * LANES] * mask[h, shift]
@@ -122,7 +150,7 @@
     def hop(distance, j, up):
         way = 0 if up else 1
         owner = row - distance if up else row + distance
-        piece = shards.at[owner, pl.ds(j * step, step)]
+        piece = shards.at[owner, span_of(j)]
         return remote(
             piece,
             piece,
@@ -135,7 +163,7 @@
     def arrival(distance, j, up):
         way = 0 if up else 1
         owner = row - distance if up else row + distance
-        piece = shards.at[owner, pl.ds(j * step, step)]
+        piece = shards.at[owner, span_of(j)]
         return remote(
             piece,
             piece,
@@ -146,8 +174,7 @@
         )
 
     def accumulate(owner, j):
-        def one(t, carry):
-            k = j * step + t
+        def one(k, carry):
             rows = []
             for i in range(batch_size):
                 shift = jnp.bitwise_xor(occ_ref[i], occ_ref[first_k + k])
@@ -159,62 +186,129 @@
             )
             return carry
 
-        lax.fori_loop(0, step, one, 0)
+        lax.fori_loop(starts[j], starts[j + 1], one, 0)
+
+    def give(j):
+        span = span_of(j)
+        return remote(
+            amp_out.at[span], amp_in.at[span], give_send.at[j], give_recv.at[j], inner_row, col
+        )
+
+    def give_away():
+        def one(k, carry):
+            for i in range(batch_size):
+                shift = jnp.bitwise_xor(occ_ref[i], occ_ref[first_k + k])
+                for h in range(SIDE // 2):
+                    g = h + SIDE // 2
+                    amp_out[k, i, :, h * LANES : (h + 1) * LANES] = (
+                        amp[h, i, k] * mask[h, shift] + amp[g, i, k] * mask[g, shift]
+                    )
+            return carry
+
+        lax.fori_loop(0, starts[len(GIVEN)], one, 0)
+
+    def accumulate_given(j):
+        def one(k, carry):
+            for c in range(SIDE):
+                h = c % (SIDE // 2)
+                rows = []
+                for i in range(batch_size):
+                    shift = jnp.bitwise_xor(occ_ref[i], occ_ref[first_k + k])
+                    rows.append(
+                        amp_in[k, i, :, h * LANES : (h + 1) * LANES] * end_mask[c, shift]
+                    )
+                end_total[...] += jnp.dot(
+                    jnp.concatenate(rows, axis=0),
+                    shards[c, k],
+                    preferred_element_type=jnp.float32,
+                )
+            return carry
+
+        lax.fori_loop(starts[j], starts[j + 1], one, 0)
+
+    def sends(distance, j, up):
+        if up:
+            there = (row >= distance) & (row < SIDE - 1)
+            return there if j >= len(GIVEN) else there & (row < SIDE - 2)
+        there = (row + distance < SIDE) & (row > 0)
+        return there if j >= len(GIVEN) else there & (row > 1)
+
+    def gets(distance, j, up):
+        if up:
+            there = row >= distance
+            return there if j >= len(GIVEN) else there & (row < SIDE - 1)
+        there = row + distance < SIDE
+        return there if j >= len(GIVEN) else there & (row > 0)
 
     for j in range(PIECES):
         raw_copies[j].wait()
-        lax.fori_loop(j * step, (j + 1) * step, fold, 0)
+        lax.fori_loop(starts[j], starts[j + 1], fold, 0)
         if j == 0:
             pl.semaphore_wait(barrier, SIDE * SIDE - 1)
-
-        @pl.when(row < SIDE - 1)
-        def _():
-            hop(0, j, True).start()
-
-        @pl.when(row > 0)
-        def _():
-            hop(0, j, False).start()
+        for up in (True, False):
+
+            @pl.when(sends(0, j, up))
+            def _():
+                hop(0, j, up).start()
 
     for copy in amp_copies:
         copy.wait()
-    for j in range(PIECES):
+
+    @pl.when(is_end)
+    def _():
+        give_away()
+
+    @pl.when(is_inner)
+    def _():
+        end_label = column_of(label_rows_ref, end_row)
+        for c in range(SIDE):
+            differ = jnp.bitwise_xor(end_label, label_rows_ref[c : c + 1, :])
+            for m in range(8):
+                end_mask[c, m] = jnp.where(differ == m, 1.0, 0.0).astype(end_mask.dtype)
+        end_total[...] = jnp.zeros_like(end_total)
+        for j in range(len(GIVEN)):
+            accumulate(row, j)
+
+    for j in range(len(GIVEN), PIECES):
         accumulate(row, j)
 
     for distance in range(1, SIDE):
         for j in range(PIECES):
-
-            @pl.when(row >= distance)
+            for up in (True, False):
+
+                @pl.when(gets(distance, j, up))
+                def _():
+                    arrival(distance, j, up).wait_recv()
+
+                if distance < SIDE - 1:
+
+                    @pl.when(sends(distance, j, up))
+                    def _():
+                        hop(distance, j, up).start()
+
+            for up in (True, False):
+
+                @pl.when(gets(distance, j, up))
+                def _():
+                    accumulate(row - distance if up else row + distance, j)
+
+        if distance == 1:
+
+            @pl.when(is_end)
             def _():
-                arrival(distance, j, True).wait_recv()
-                if distance < SIDE - 1:
-
-                    @pl.when(row < SIDE - 1)
-                    def _():
-                        hop(distance, j, True).start()
-
-            @pl.when(row + distance < SIDE)
-            def _():
-                arrival(distance, j, False).wait_recv()
-                if distance < SIDE - 1:
-
-                    @pl.when(row > 0)
-                    def _():
-                        hop(distance, j, False).start()
-
-            @pl.when(row >= distance)
-            def _():
-                accumulate(row - distance, j)
-
-            @pl.when(row + distance < SIDE)
-            def _():
-                accumulate(row + distance, j)
+                for j in range(len(GIVEN)):
+                    give(j).start()
 
     share = total.shape[0] // SIDE
+
+    def own_rows(ref, to_col):
+        return ref.at[pl.ds(pl.multiple_of(to_col * share, share), share)]
+
     col_copies = []
     for ahead in range(1, SIDE):
         to_col = lax.rem(col + ahead, SIDE)
         copy = remote(
-            total.at[pl.ds(pl.multiple_of(to_col * share, share), share)],
+            own_rows(total, to_col),
             from_cols.at[ahead - 1],
             col_send.at[ahead - 1],
             col_recv.at[ahead - 1],
@@ -223,10 +317,46 @@
         )
         copy.start()
         col_copies.append(copy)
+
+    def end_col_copy(ahead):
+        to_col = lax.rem(col + ahead, SIDE)
+        return remote(
+            own_rows(end_total, to_col),
+            end_cols.at[ahead - 1],
+            give_col_send.at[ahead - 1],
+            give_col_recv.at[ahead - 1],
+            row,
+            to_col,
+        )
+
+    def give_back():
+        return remote(end_sum, from_inner, back_send, back_recv, end_row, col)
+
+    @pl.when(is_inner)
+    def _():
+        for j in range(len(GIVEN)):
+            give(j).wait_recv()
+            accumulate_given(j)
+        for ahead in range(1, SIDE):
+            end_col_copy(ahead).start()
+        summed = end_total[pl.ds(pl.multiple_of(col * share, share), share), :]
+        for ahead in range(1, SIDE):
+            end_col_copy(ahead).wait_recv()
+            summed += end_cols[ahead - 1]
+        end_sum[...] = summed
+        give_back().start()
+        from_inner[...] = jnp.zeros_like(from_inner)
+
     summed = total[pl.ds(pl.multiple_of(col * share, share), share), :]
     for ahead in range(1, SIDE):
         col_copies[ahead - 1].wait_recv()
         summed += from_cols[ahead - 1]
+
+    @pl.when(is_end)
+    def _():
+        give_back().wait_recv()
+
+    summed += from_inner[...]
     halves[0] = summed[:, :LANES]
     halves[1] = summed[:, LANES:]
 
@@ -262,13 +392,21 @@
             col,
         )
 
+    energy_of_a = energy_rows_ref[pl.ds(col, 1), :]
+    energy_of_b = column_of(energy_rows_ref, row)
+    wanted = jnp.bitwise_xor(
+        jnp.bitwise_xor(row_label, label_rows_ref[pl.ds(col, 1), :]), occ_ref[batch_size]
+    )
     for i in range(SIDE):
 
         @pl.when((row != col) | (col != i))
         def _():
             delivered(i).wait_recv()
 
-        out_ref[i] = landed[i]
+        value = jnp.where(wanted == occ_ref[i], landed[i].T, 0.0)
+        out_ref[:, i, :] = value / (
+            occ_energy_ref[i] + occ_energy_ref[batch_size] - energy_of_a - energy_of_b
+        )
 
     for ahead in range(1, SIDE):
         col_copies[ahead - 1].wait_send()
@@ -280,35 +418,42 @@
 
     for distance in range(SIDE - 1):
         for j in range(PIECES):
-
-            @pl.when((row >= distance) & (row < SIDE - 1))
-            def _():
-                hop(distance, j, True).wait_send()
-
-            @pl.when((row + distance < SIDE) & (row > 0))
-            def _():
-                hop(distance, j, False).wait_send()
-
-
-def cycle_blocks(amplitudes, integrals, occ_irrep, vir_irrep, vir_local, screen):
+            for up in (True, False):
+
+                @pl.when(sends(distance, j, up))
+                def _():
+                    hop(distance, j, up).wait_send()
+
+    @pl.when(is_end)
+    def _():
+        for j in range(len(GIVEN)):
+            give(j).wait_send()
+
+    @pl.when(is_inner)
+    def _():
+        for ahead in range(1, SIDE):
+            end_col_copy(ahead).wait_send()
+        give_back().wait_send()
+
+
+def cycle_blocks(
+    amplitudes, integrals, occ_irrep, vir_irrep, screen, occ_energy, vir_energy
+):
     batch_size, occ_share, vir_share, vir_total = amplitudes.shape
     half = vir_total // 2
     bf16, f32 = jnp.bfloat16, jnp.float32
-    step = occ_share // PIECES
-    vmem, smem = pltpu.VMEM, pltpu.SMEM
+    given = sum(GIVEN)
+    sizes = GIVEN + ((occ_share - given) // OWN,) * OWN
+    vmem, smem, dma = pltpu.VMEM, pltpu.SMEM, pltpu.SemaphoreType.DMA
     hops = (2, SIDE - 1, PIECES)
+    in_vmem = pl.BlockSpec(memory_space=vmem)
+    in_smem = pl.BlockSpec(memory_space=smem)
+    anywhere = pl.BlockSpec(memory_space=pl.ANY)
     return pl.pallas_call(
-        functools.partial(cycle_kernel, step),
-        out_shape=jax.ShapeDtypeStruct((batch_size, LANES, LANES), f32),
-        in_specs=[
-            pl.BlockSpec(memory_space=smem),
-            pl.BlockSpec(memory_space=smem),
-            pl.BlockSpec(memory_space=vmem),
-            pl.BlockSpec(memory_space=vmem),
-            pl.BlockSpec(memory_space=pl.ANY),
-            pl.BlockSpec(memory_space=pl.ANY),
-        ],
-        out_specs=pl.BlockSpec(memory_space=vmem),
+        functools.partial(cycle_kernel, sizes),
+        out_shape=jax.ShapeDtypeStruct((LANES, batch_size, LANES), f32),
+        in_specs=[in_smem, in_smem, in_smem, in_vmem, in_vmem, anywhere, anywhere],
+        out_specs=in_vmem,
         scratch_shapes=[
             vmem((occ_share, vir_share, vir_total), bf16),
             vmem((SIDE, batch_size, occ_share, vir_share, LANES), bf16),
@@ -319,24 +464,38 @@
             vmem((SIDE - 1, vir_share, half), f32),
             vmem((2, vir_share, LANES), f32),
             vmem((SIDE, vir_share, LANES), f32),
-            pltpu.SemaphoreType.DMA((PIECES,)),
-            pltpu.SemaphoreType.DMA((SIDE,)),
-            pltpu.SemaphoreType.DMA(hops),
-            pltpu.SemaphoreType.DMA(hops),
-            pltpu.SemaphoreType.DMA((SIDE - 1,)),
-            pltpu.SemaphoreType.DMA((SIDE - 1,)),
-            pltpu.SemaphoreType.DMA((SIDE,)),
-            pltpu.SemaphoreType.DMA((SIDE,)),
+            vmem((SIDE, 8, vir_share, LANES), bf16),
+            vmem((given, batch_size, vir_share, half), bf16),
+            vmem((given, batch_size, vir_share, half), bf16),
+            vmem((batch_size * vir_share, half), f32),
+            vmem((SIDE - 1, vir_share, half), f32),
+            vmem((vir_share, half), f32),
+            vmem((vir_share, half), f32),
+            dma((PIECES,)),
+            dma((SIDE,)),
+            dma(hops),
+            dma(hops),
+            dma((SIDE - 1,)),
+            dma((SIDE - 1,)),
+            dma((SIDE,)),
+            dma((SIDE,)),
+            dma((len(GIVEN),)),
+            dma((len(GIVEN),)),
+            dma((SIDE - 1,)),
+            dma((SIDE - 1,)),
+            dma,
+            dma,
         ],
         compiler_params=pltpu.CompilerParams(
-            collective_id=0, has_side_effects=True, vmem_limit_bytes=48 * 1024 * 1024
+            collective_id=0, has_side_effects=True, vmem_limit_bytes=52 * 1024 * 1024
         ),
         name="cycle_blocks",
     )(
         occ_irrep,
-        screen.reshape(-1),
+        screen,
+        occ_energy,
         vir_irrep.reshape(SIDE, LANES),
-        jnp.broadcast_to(vir_local[:, None], (vir_share, LANES)),
+        vir_energy.reshape(SIDE, LANES),
         integrals,
         amplitudes,
     )
@@ -348,7 +507,8 @@
         row_count == column_count == batch_size == SIDE
         and vir_share == LANES
         and vir_total == SIDE * LANES
-        and occ_share % PIECES == 0
+        and occ_share > sum(GIVEN)
+        and (occ_share - sum(GIVEN)) % OWN == 0
     )
 
 
@@ -357,6 +517,10 @@
     column_count = lax.axis_size("col")
     row, col = lax.axis_index("row"), lax.axis_index("col")
     batch_size, occ_share, vir_share, vir_total = amplitudes.shape
+    if fits_kernel(row_count, column_count, amplitudes):
+        return cycle_blocks(
+            amplitudes, integrals, occ_irrep, vir_irrep, screen, occ_energy, vir_energy
+        )
     half = vir_total // 2
     vir_columns = vir_total // column_count
     occ_offset = col * occ_share
@@ -365,25 +529,22 @@
     screen_rows = lax.dynamic_slice_in_dim(screen, occ_offset, occ_share, 0)
     pair_label = occ_irrep[batch_size]
 
-    if fits_kernel(row_count, column_count, amplitudes):
-        cycle = cycle_blocks(amplitudes, integrals, occ_irrep, vir_irrep, vir_local, screen)
-    else:
-        folded = folded_integrals(
-            integrals, occ_local, vir_local, vir_irrep, screen_rows, pair_label
-        )
-        gathered = lax.all_gather(folded, "row", axis=1, tiled=True)
-        shift = jnp.bitwise_xor(occ_irrep[:batch_size, None], occ_local[None, :])
-        keep_amp = (
-            jnp.bitwise_xor(shift[:, :, None], vir_local[None, None, :])[:, :, :, None]
-            == vir_irrep[None, None, None, :]
-        )
-        amp_kept = jnp.where(keep_amp, amplitudes, jnp.zeros_like(amplitudes))
-        partial = lax.dot_general(
-            amp_kept, gathered, (((1, 3), (0, 1)), ((), ())), preferred_element_type=jnp.float32
-        )
-        whole = lax.all_gather(lax.psum(partial, "col"), "row", axis=1, tiled=True)
-        cycle = lax.dynamic_slice_in_dim(whole, col * vir_columns, vir_columns, 1)
-        cycle = lax.dynamic_slice_in_dim(cycle, (row * vir_share) % half, vir_share, 2)
+    folded = folded_integrals(
+        integrals, occ_local, vir_local, vir_irrep, screen_rows, pair_label
+    )
+    gathered = lax.all_gather(folded, "row", axis=1, tiled=True)
+    shift = jnp.bitwise_xor(occ_irrep[:batch_size, None], occ_local[None, :])
+    keep_amp = (
+        jnp.bitwise_xor(shift[:, :, None], vir_local[None, None, :])[:, :, :, None]
+        == vir_irrep[None, None, None, :]
+    )
+    amp_kept = jnp.where(keep_amp, amplitudes, jnp.zeros_like(amplitudes))
+    partial = lax.dot_general(
+        amp_kept, gathered, (((1, 3), (0, 1)), ((), ())), preferred_element_type=jnp.float32
+    )
+    whole = lax.all_gather(lax.psum(partial, "col"), "row", axis=1, tiled=True)
+    cycle = lax.dynamic_slice_in_dim(whole, col * vir_columns, vir_columns, 1)
+    cycle = lax.dynamic_slice_in_dim(cycle, (row * vir_share) % half, vir_share, 2)
     cycle = jnp.transpose(cycle, (2, 0, 1))
     col_irrep = lax.dynamic_slice_in_dim(vir_irrep, col * vir_columns, vir_columns)
     kept = (

time: 141 us -> 107 us (0.76)
  Pallas kernels: 129 us -> 102 us
  local copies, waits for them, and re-layouts: 8.37 us -> 4.17 us
  other arithmetic: 3.75 us -> 0 us
    pallas_call x1, Pallas kernels: 129 us -> 102 us  [cycle_blocks(): pl.pallas_call(functools.partial(cycle_kernel, sizes), out_shape=jax.Shap...]
    slice x2 -> x0, local copies, waits for them, and re-layouts: 2.48 us -> none  [the longest x1 1.24 us: on_device(): occ_energy[batch_size]]
    xor x2 -> x0, other arithmetic: 2.2 us -> none  [the longest x1 1.48 us: on_device(): pair_label ^ col_irrep[None, :]]
    unnamed x7 -> x10, local copies, waits for them, and re-layouts: 4.06 us -> 4.17 us
where the time goes in v3:
time: 107 us; the launch traced here: 106 us
  Pallas kernels  102 us (95%)
  local copies, waits for them, and re-layouts  4.17 us (4%)
    pallas_call x1, Pallas kernels, cycle_blocks(): pl.pallas_call(functools.partial(cycle_kernel, sizes), out_shape=jax.Shap...  102 us
    unnamed x10, local copies, waits for them, and re-layouts  4.17 us

profile of v3, /device:TPU:24, one launch (start us, length us, event | category | flops | bytes accessed | tf_op | source)
XLA Modules:
  0.0 106.4 jit_solution(4285272222719658668)
XLA Ops:
  0.0 0.8 copy.8.screen_ref
  0.8 0.0 copy-start
  0.8 0.7 copy-done
  1.5 0.0 copy-start.1
  1.5 0.7 copy-done.1
  2.2 0.0 copy-start.2
  2.2 0.7 copy-done.2
  2.8 0.0 copy-start.3
  2.8 0.7 copy-done.3
  3.5 102.2 %cycle_blocks.1 = f32[128,4,128]{2,1,0:T(4,128)S(1)} custom-call(s32[100]{0:T(128)S(1)} %copy-done.2, s32[100,8]{1,0:T(8,128)S(1)} %copy.8.screen_ref, f32[100]{0:T(128)S(1)} %copy-done.3, s32[4,128]{1,0:T(4,128)S(1)} %bitcast.2, f32[4,128]{1,0:T(4,128)S(1)} %bitcast.3, bf16[25,128,512]{2,1,0:T(8,128)(2,1)} %int_hbm.1, bf16[4,25,128,512]{3,2,1,0:T(8,128)(2,1)} %amp_hbm.1), custom_call_target="tpu_custom_call" | custom-call | tf_op jit(solution)/shard_map/cycle_blocks/pallas_call | solution.py:452
  105.7 0.7 copy.10
Async XLA Ops:
  0.8 0.7 copy-start
  1.5 0.7 copy-start.1
  2.2 0.7 copy-start.2
  2.8 0.7 copy-start.3

commit v4 on v3

--- a/solution.py
+++ b/solution.py
@@ -11,7 +11,7 @@
 SIDE = 4
 GIVEN = (4, 3)
 OWN = 3
-PIECES = len(GIVEN) + OWN
+PIECES = OWN + len(GIVEN)
 
 
 def folded_integrals(integrals, occ_local, vir_local, vir_irrep, screen_rows, pair_label):
@@ -189,9 +189,14 @@
         lax.fori_loop(starts[j], starts[j + 1], one, 0)
 
     def give(j):
-        span = span_of(j)
-        return remote(
-            amp_out.at[span], amp_in.at[span], give_send.at[j], give_recv.at[j], inner_row, col
+        span = pl.ds(starts[j] - starts[OWN], sizes[j])
+        return remote(
+            amp_out.at[span],
+            amp_in.at[span],
+            give_send.at[j - OWN],
+            give_recv.at[j - OWN],
+            inner_row,
+            col,
         )
 
     def give_away():
@@ -200,12 +205,12 @@
                 shift = jnp.bitwise_xor(occ_ref[i], occ_ref[first_k + k])
                 for h in range(SIDE // 2):
                     g = h + SIDE // 2
-                    amp_out[k, i, :, h * LANES : (h + 1) * LANES] = (
+                    amp_out[k - starts[OWN], i, :, h * LANES : (h + 1) * LANES] = (
                         amp[h, i, k] * mask[h, shift] + amp[g, i, k] * mask[g, shift]
                     )
             return carry
 
-        lax.fori_loop(0, starts[len(GIVEN)], one, 0)
+        lax.fori_loop(starts[OWN], starts[PIECES], one, 0)
 
     def accumulate_given(j):
         def one(k, carry):
@@ -215,7 +220,8 @@
                 for i in range(batch_size):
                     shift = jnp.bitwise_xor(occ_ref[i], occ_ref[first_k + k])
                     rows.append(
-                        amp_in[k, i, :, h * LANES : (h + 1) * LANES] * end_mask[c, shift]
+                        amp_in[k - starts[OWN], i, :, h * LANES : (h + 1) * LANES]
+                        * end_mask[c, shift]
                     )
                 end_total[...] += jnp.dot(
                     jnp.concatenate(rows, axis=0),
@@ -229,16 +235,16 @@
     def sends(distance, j, up):
         if up:
             there = (row >= distance) & (row < SIDE - 1)
-            return there if j >= len(GIVEN) else there & (row < SIDE - 2)
+            return there if j < OWN else there & (row < SIDE - 2)
         there = (row + distance < SIDE) & (row > 0)
-        return there if j >= len(GIVEN) else there & (row > 1)
+        return there if j < OWN else there & (row > 1)
 
     def gets(distance, j, up):
         if up:
             there = row >= distance
-            return there if j >= len(GIVEN) else there & (row < SIDE - 1)
+            return there if j < OWN else there & (row < SIDE - 1)
         there = row + distance < SIDE
-        return there if j >= len(GIVEN) else there & (row > 0)
+        return there if j < OWN else there & (row > 0)
 
     for j in range(PIECES):
         raw_copies[j].wait()
@@ -266,10 +272,10 @@
             for m in range(8):
                 end_mask[c, m] = jnp.where(differ == m, 1.0, 0.0).astype(end_mask.dtype)
         end_total[...] = jnp.zeros_like(end_total)
-        for j in range(len(GIVEN)):
+        for j in range(OWN, PIECES):
             accumulate(row, j)
 
-    for j in range(len(GIVEN), PIECES):
+    for j in range(OWN):
         accumulate(row, j)
 
     for distance in range(1, SIDE):
@@ -296,91 +302,84 @@
 
             @pl.when(is_end)
             def _():
-                for j in range(len(GIVEN)):
+                for j in range(OWN, PIECES):
                     give(j).start()
 
     share = total.shape[0] // SIDE
 
-    def own_rows(ref, to_col):
-        return ref.at[pl.ds(pl.multiple_of(to_col * share, share), share)]
-
-    col_copies = []
-    for ahead in range(1, SIDE):
+    def own_rows(to_col):
+        return pl.ds(pl.multiple_of(to_col * share, share), share)
+
+    def col_copy(source, target, send, recv, h, ahead):
         to_col = lax.rem(col + ahead, SIDE)
-        copy = remote(
-            own_rows(total, to_col),
-            from_cols.at[ahead - 1],
-            col_send.at[ahead - 1],
-            col_recv.at[ahead - 1],
+        return remote(
+            source.at[own_rows(to_col), pl.ds(h * LANES, LANES)],
+            target.at[ahead - 1, h],
+            send.at[h, ahead - 1],
+            recv.at[h, ahead - 1],
             row,
             to_col,
         )
-        copy.start()
-        col_copies.append(copy)
-
-    def end_col_copy(ahead):
-        to_col = lax.rem(col + ahead, SIDE)
-        return remote(
-            own_rows(end_total, to_col),
-            end_cols.at[ahead - 1],
-            give_col_send.at[ahead - 1],
-            give_col_recv.at[ahead - 1],
-            row,
-            to_col,
-        )
-
-    def give_back():
-        return remote(end_sum, from_inner, back_send, back_recv, end_row, col)
+
+    own_copy = functools.partial(col_copy, total, from_cols, col_send, col_recv)
+    end_copy = functools.partial(col_copy, end_total, end_cols, give_col_send, give_col_recv)
+
+    def give_back(h):
+        return remote(
+            end_sum.at[h], from_inner.at[h], back_send.at[h], back_recv.at[h], end_row, col
+        )
+
+    for h in range(2):
+        for ahead in range(1, SIDE):
+            own_copy(h, ahead).start()
 
     @pl.when(is_inner)
     def _():
-        for j in range(len(GIVEN)):
+        for j in range(OWN, PIECES):
             give(j).wait_recv()
             accumulate_given(j)
-        for ahead in range(1, SIDE):
-            end_col_copy(ahead).start()
-        summed = end_total[pl.ds(pl.multiple_of(col * share, share), share), :]
-        for ahead in range(1, SIDE):
-            end_col_copy(ahead).wait_recv()
-            summed += end_cols[ahead - 1]
-        end_sum[...] = summed
-        give_back().start()
+        for h in range(2):
+            for ahead in range(1, SIDE):
+                end_copy(h, ahead).start()
+        for h in range(2):
+            summed = end_total[own_rows(col), h * LANES : (h + 1) * LANES]
+            for ahead in range(1, SIDE):
+                end_copy(h, ahead).wait_recv()
+                summed += end_cols[ahead - 1, h]
+            end_sum[h] = summed
+            give_back(h).start()
         from_inner[...] = jnp.zeros_like(from_inner)
 
-    summed = total[pl.ds(pl.multiple_of(col * share, share), share), :]
-    for ahead in range(1, SIDE):
-        col_copies[ahead - 1].wait_recv()
-        summed += from_cols[ahead - 1]
-
-    @pl.when(is_end)
-    def _():
-        give_back().wait_recv()
-
-    summed += from_inner[...]
-    halves[0] = summed[:, :LANES]
-    halves[1] = summed[:, LANES:]
-
-    def deliver(ahead):
-        to_row = lax.rem(row + ahead, SIDE)
-        return remote(
-            halves.at[lax.rem(to_row, 2)],
+    def deliver(to_row):
+        return remote(
+            halves.at[to_row % 2],
             landed.at[col],
-            end_send.at[ahead],
+            end_send.at[to_row],
             end_recv.at[col],
             to_row,
             row,
         )
 
-    for ahead in range(1, SIDE):
-        deliver(ahead).start()
-
-    @pl.when(row != col)
-    def _():
-        deliver(0).start()
-
-    @pl.when(row == col)
-    def _():
-        landed[col] = halves[lax.rem(row, 2)]
+    for h in range(2):
+        summed = total[own_rows(col), h * LANES : (h + 1) * LANES]
+        for ahead in range(1, SIDE):
+            own_copy(h, ahead).wait_recv()
+            summed += from_cols[ahead - 1, h]
+
+        @pl.when(is_end)
+        def _():
+            give_back(h).wait_recv()
+
+        halves[h] = summed + from_inner[h]
+        for to_row in (h, h + 2):
+
+            @pl.when((row != to_row) | (col != to_row))
+            def _():
+                deliver(to_row).start()
+
+            @pl.when((row == to_row) & (col == to_row))
+            def _():
+                landed[to_row] = halves[h]
 
     def delivered(i):
         return remote(
@@ -408,13 +407,14 @@
             occ_energy_ref[i] + occ_energy_ref[batch_size] - energy_of_a - energy_of_b
         )
 
-    for ahead in range(1, SIDE):
-        col_copies[ahead - 1].wait_send()
-        deliver(ahead).wait_send()
-
-    @pl.when(row != col)
-    def _():
-        deliver(0).wait_send()
+    for h in range(2):
+        for ahead in range(1, SIDE):
+            own_copy(h, ahead).wait_send()
+    for to_row in range(SIDE):
+
+        @pl.when((row != to_row) | (col != to_row))
+        def _():
+            deliver(to_row).wait_send()
 
     for distance in range(SIDE - 1):
         for j in range(PIECES):
@@ -426,14 +426,15 @@
 
     @pl.when(is_end)
     def _():
-        for j in range(len(GIVEN)):
+        for j in range(OWN, PIECES):
             give(j).wait_send()
 
     @pl.when(is_inner)
     def _():
-        for ahead in range(1, SIDE):
-            end_col_copy(ahead).wait_send()
-        give_back().wait_send()
+        for h in range(2):
+            for ahead in range(1, SIDE):
+                end_copy(h, ahead).wait_send()
+            give_back(h).wait_send()
 
 
 def cycle_blocks(
@@ -443,7 +444,7 @@
     half = vir_total // 2
     bf16, f32 = jnp.bfloat16, jnp.float32
     given = sum(GIVEN)
-    sizes = GIVEN + ((occ_share - given) // OWN,) * OWN
+    sizes = ((occ_share - given) // OWN,) * OWN + GIVEN
     vmem, smem, dma = pltpu.VMEM, pltpu.SMEM, pltpu.SemaphoreType.DMA
     hops = (2, SIDE - 1, PIECES)
     in_vmem = pl.BlockSpec(memory_space=vmem)
@@ -461,30 +462,30 @@
             vmem((8, vir_share, LANES), f32),
             vmem((SIDE, occ_share, vir_share, half), bf16),
             vmem((batch_size * vir_share, half), f32),
-            vmem((SIDE - 1, vir_share, half), f32),
+            vmem((SIDE - 1, 2, vir_share, LANES), f32),
             vmem((2, vir_share, LANES), f32),
             vmem((SIDE, vir_share, LANES), f32),
             vmem((SIDE, 8, vir_share, LANES), bf16),
             vmem((given, batch_size, vir_share, half), bf16),
             vmem((given, batch_size, vir_share, half), bf16),
             vmem((batch_size * vir_share, half), f32),
-            vmem((SIDE - 1, vir_share, half), f32),
-            vmem((vir_share, half), f32),
-            vmem((vir_share, half), f32),
+            vmem((SIDE - 1, 2, vir_share, LANES), f32),
+            vmem((2, vir_share, LANES), f32),
+            vmem((2, vir_share, LANES), f32),
             dma((PIECES,)),
             dma((SIDE,)),
             dma(hops),
             dma(hops),
-            dma((SIDE - 1,)),
-            dma((SIDE - 1,)),
+            dma((2, SIDE - 1)),
+            dma((2, SIDE - 1)),
             dma((SIDE,)),
             dma((SIDE,)),
             dma((len(GIVEN),)),
             dma((len(GIVEN),)),
-            dma((SIDE - 1,)),
-            dma((SIDE - 1,)),
-            dma,
-            dma,
+            dma((2, SIDE - 1)),
+            dma((2, SIDE - 1)),
+            dma((2,)),
+            dma((2,)),
         ],
         compiler_params=pltpu.CompilerParams(
             collective_id=0, has_side_effects=True, vmem_limit_bytes=52 * 1024 * 1024

time: 107 us -> 107 us (level)
  no operation moved by 1% of the time
where the time goes in v4:
time: 107 us
  Pallas kernels  102 us (95%)
  local copies, waits for them, and re-layouts  4.17 us (4%)
    pallas_call x1, Pallas kernels, cycle_blocks(): pl.pallas_call(functools.partial(cycle_kernel, sizes), out_shape=jax.Shap...  102 us
    unnamed x10, local copies, waits for them, and re-layouts  4.17 us

profile of v4, /device:TPU:24, one launch (start us, length us, event | category | flops | bytes accessed | tf_op | source)
XLA Modules:
  0.0 106.5 jit_solution(1679768521381963783)
XLA Ops:
  0.0 0.8 copy.8.screen_ref
  0.8 0.0 copy-start
  0.8 0.7 copy-done
  1.5 0.0 copy-start.1
  1.5 0.7 copy-done.1
  2.2 0.0 copy-start.2
  2.2 0.7 copy-done.2
  2.8 0.0 copy-start.3
  2.8 0.7 copy-done.3
  3.5 102.3 %cycle_blocks.1 = f32[128,4,128]{2,1,0:T(4,128)S(1)} custom-call(s32[100]{0:T(128)S(1)} %copy-done.2, s32[100,8]{1,0:T(8,128)S(1)} %copy.8.screen_ref, f32[100]{0:T(128)S(1)} %copy-done.3, s32[4,128]{1,0:T(4,128)S(1)} %bitcast.2, f32[4,128]{1,0:T(4,128)S(1)} %bitcast.3, bf16[25,128,512]{2,1,0:T(8,128)(2,1)} %int_hbm.1, bf16[4,25,128,512]{3,2,1,0:T(8,128)(2,1)} %amp_hbm.1), custom_call_target="tpu_custom_call" | custom-call | tf_op jit(solution)/shard_map/cycle_blocks/pallas_call | solution.py:453
  105.8 0.7 copy.10
Async XLA Ops:
  0.8 0.7 copy-start
  1.5 0.7 copy-start.1
  2.2 0.7 copy-start.2
  2.8 0.7 copy-start.3

commit v5 on v4

--- a/solution.py
+++ b/solution.py
@@ -30,14 +30,19 @@
 
 def cycle_kernel(
     sizes,
+    screen_ref,
+    occ_hbm,
+    occ_energy_hbm,
+    label_rows_hbm,
+    energy_rows_hbm,
+    int_hbm,
+    amp_hbm,
+    out_ref,
     occ_ref,
-    screen_ref,
     occ_energy_ref,
     label_rows_ref,
     energy_rows_ref,
-    int_hbm,
-    amp_hbm,
-    out_ref,
+    small_sem,
     raw,
     amp,
     mask,
@@ -96,6 +101,18 @@
             device_id_type=pl.DeviceIdType.MESH,
         )
 
+    small_copies = []
+    for n, (source, target) in enumerate(
+        (
+            (occ_hbm, occ_ref),
+            (label_rows_hbm, label_rows_ref),
+            (occ_energy_hbm, occ_energy_ref),
+            (energy_rows_hbm, energy_rows_ref),
+        )
+    ):
+        copy = pltpu.make_async_copy(source, target, small_sem.at[n])
+        copy.start()
+        small_copies.append(copy)
     raw_copies = []
     for j in range(PIECES):
         span = span_of(j)
@@ -125,6 +142,8 @@
                     device_id_type=pl.DeviceIdType.MESH,
                 )
 
+    for copy in small_copies:
+        copy.wait()
     row_label = column_of(label_rows_ref, row)
     for c in range(SIDE):
         differ = jnp.bitwise_xor(row_label, label_rows_ref[c : c + 1, :])
@@ -214,20 +233,22 @@
 
     def accumulate_given(j):
         def one(k, carry):
-            for c in range(SIDE):
-                h = c % (SIDE // 2)
-                rows = []
-                for i in range(batch_size):
-                    shift = jnp.bitwise_xor(occ_ref[i], occ_ref[first_k + k])
-                    rows.append(
+            rows = []
+            for i in range(batch_size):
+                shift = jnp.bitwise_xor(occ_ref[i], occ_ref[first_k + k])
+                blocks = []
+                for c in range(SIDE):
+                    h = c % (SIDE // 2)
+                    blocks.append(
                         amp_in[k - starts[OWN], i, :, h * LANES : (h + 1) * LANES]
                         * end_mask[c, shift]
                     )
-                end_total[...] += jnp.dot(
-                    jnp.concatenate(rows, axis=0),
-                    shards[c, k],
-                    preferred_element_type=jnp.float32,
-                )
+                rows.append(jnp.concatenate(blocks, axis=1))
+            end_total[...] += jnp.dot(
+                jnp.concatenate(rows, axis=0),
+                jnp.concatenate([shards[c, k] for c in range(SIDE)], axis=0),
+                preferred_element_type=jnp.float32,
+            )
             return carry
 
         lax.fori_loop(starts[j], starts[j + 1], one, 0)
@@ -453,9 +474,14 @@
     return pl.pallas_call(
         functools.partial(cycle_kernel, sizes),
         out_shape=jax.ShapeDtypeStruct((LANES, batch_size, LANES), f32),
-        in_specs=[in_smem, in_smem, in_smem, in_vmem, in_vmem, anywhere, anywhere],
+        in_specs=[in_smem] + [anywhere] * 6,
         out_specs=in_vmem,
         scratch_shapes=[
+            smem(occ_irrep.shape, occ_irrep.dtype),
+            smem(occ_energy.shape, f32),
+            vmem((SIDE, LANES), vir_irrep.dtype),
+            vmem((SIDE, LANES), f32),
+            dma((4,)),
             vmem((occ_share, vir_share, vir_total), bf16),
             vmem((SIDE, batch_size, occ_share, vir_share, LANES), bf16),
             vmem((SIDE, 8, vir_share, LANES), bf16),
@@ -488,12 +514,12 @@
             dma((2,)),
         ],
         compiler_params=pltpu.CompilerParams(
-            collective_id=0, has_side_effects=True, vmem_limit_bytes=52 * 1024 * 1024
+            collective_id=0, has_side_effects=True, vmem_limit_bytes=64 * 1024 * 1024
         ),
         name="cycle_blocks",
     )(
+        screen,
         occ_irrep,
-        screen,
         occ_energy,
         vir_irrep.reshape(SIDE, LANES),
         vir_energy.reshape(SIDE, LANES),

time: 107 us -> 109 us (1.019)
  Pallas kernels: 102 us -> 105 us
    pallas_call x1, Pallas kernels: 102 us -> 105 us  [cycle_blocks(): pl.pallas_call(functools.partial(cycle_kernel, sizes), out_shape=jax.Shap...]
    unnamed x10 -> x2, local copies, waits for them, and re-layouts: 4.17 us -> 3.08 us
where the time goes in v5:
time: 109 us; the launch traced here: 108 us
  Pallas kernels  105 us (96%)
  local copies, waits for them, and re-layouts  3.08 us (3%)
    pallas_call x1, Pallas kernels, cycle_blocks(): pl.pallas_call(functools.partial(cycle_kernel, sizes), out_shape=jax.Shap...  105 us
    unnamed x2, local copies, waits for them, and re-layouts  3.08 us

profile of v5, /device:TPU:24, one launch (start us, length us, event | category | flops | bytes accessed | tf_op | source)
XLA Modules:
  0.0 108.5 jit_solution(612302713694195195)
XLA Ops:
  0.0 1.4 %copy.8.screen_ref = s32[100,8]{1,0:T(8,128)} copy(s32[100,8]{0,1:T(8,128)} %param.11) | data formatting | bytes 6400 | tf_op args[4]
  1.4 105.4 %cycle_blocks.1 = f32[128,4,128]{2,1,0:T(4,128)} custom-call(s32[100,8]{1,0:T(8,128)} %copy.8.screen_ref, s32[100]{0:T(128)} %occ_hbm.1, f32[100]{0:T(128)} %occ_energy_hbm.1, s32[4,128]{1,0:T(4,128)} %bitcast.2, f32[4,128]{1,0:T(4,128)} %bitcast.3, bf16[25,128,512]{2,1,0:T(8,128)(2,1)} %int_hbm.1, bf16[4,25,128,512]{3,2,1,0:T(8,128)(2,1)} %amp_hbm.1), custom_call_target="tpu_custom_call" | custom-call | tf_op jit(solution)/shard_map/cycle_blocks/pallas_call | solution.py:474
  106.8 1.7 %copy.10 = f32[128,4,128]{2,1,0:T(4,128)} copy(f32[128,4,128]{2,1,0:T(4,128)} %cycle_blocks.1) | data formatting | bytes 524288
